TPU v7x, 32 devices: a whole 2x2x4 slice. The times are simulated.
32 devices in a mesh: term: 4 (over y, x), sector: 8 (over z, core).
Axes of the slice: x: 2, y: 2, z: 4, core: 2. Of those that a mesh axis runs over, the one named last changes fastest.
Arguments:
- psi: bfloat16 [8, 8, 128, 128], P('sector'), may hold values from -6 to 6
- left_env: bfloat16 [8, 8, 128, 128], P('term', 'sector'), may hold values from -40 to 40
- right_env: bfloat16 [8, 8, 128, 128], P('term', 'sector'), may hold values from -4 to 4
- precond: bfloat16 [8, 8, 128, 128], P('sector'), may hold values from 0.5 to 4
- block_sizes: int32 [8], replicated, may hold values from 32 to 128, as said below
Outputs:
- state: bfloat16 [8, 8, 128, 128], P('sector')
- energy: float32 [3], replicated
Inputs may be any that keep to these rules, and one draw needn't show every extreme that they name: `block_sizes`: some sector has exactly 128 rows in every draw.
All inputs are finite; a program needn't handle non-finite values.
Results may differ from a plain program's by a relative error of at most 0.022.
Values may be sent and summed in bfloat16 or wider, within the bound.
No kernel may reach another device: no remote copies, remote signals or barrier semaphores. Data moves between devices by JAX's collectives and lax.ppermute only.
A program may use at most 128 MiB of HBM per device.

v0:
```python
import jax
import jax.numpy as jnp
from jax import lax
from jax.sharding import PartitionSpec as P

ITERS = 3


def block_mask(block_sizes, width, own_row):
    rows = jnp.arange(width)
    valid = rows[None, :] < block_sizes[:, None]
    own_valid = lax.dynamic_slice_in_dim(valid, own_row, 1, 0)[0]
    return (own_valid[None, :, None] & valid[:, None, :]).astype(jnp.float32)


def dot_sums(cur_share, img_share, pre_share, count):
    first = lax.psum(
        (jnp.sum(cur_share * cur_share), jnp.sum(cur_share * img_share)), ("term", "sector")
    )
    theta = first[1] / first[0]
    fresh = cur_share - (img_share - theta * cur_share) / pre_share
    squares = lax.psum(jnp.sum(fresh * fresh), ("term", "sector"))
    return (theta, lax.rsqrt(squares / count + 1e-06))


def local(psi, left_env, right_env, precond, block_sizes):
    sectors = block_sizes.shape[0]
    width = psi.shape[-1]
    own_row = lax.axis_index("sector")
    share = sectors // lax.axis_size("term")
    share_start = lax.axis_index("term") * share
    count = float(sectors * sectors * width * width)
    mask = block_mask(block_sizes, width, own_row)
    state = (psi[0].astype(jnp.float32) * mask).astype(jnp.bfloat16)
    scaling = precond[0].astype(jnp.float32)
    left_own = left_env[:, 0]

    def portion(values):
        return lax.dynamic_slice_in_dim(values, share_start, share, 0)

    right_all = lax.all_gather(right_env, "sector", axis=1, tiled=True)
    energies = []
    for step in range(ITERS):
        images = jnp.einsum(
            "jab,kjcb->kjac", state, right_all, preferred_element_type=jnp.float32
        ).astype(jnp.bfloat16)
        partial_value = jnp.einsum(
            "kac,kjcd->jad", left_own, images, preferred_element_type=jnp.float32
        )
        current = state.astype(jnp.float32)
        image = lax.psum(partial_value.astype(jnp.bfloat16), "term").astype(jnp.float32) * mask
        theta, factor = dot_sums(portion(current), portion(image), portion(scaling), count)
        fresh = current - (image - theta * current) / scaling
        state = (fresh * factor).astype(jnp.bfloat16)
        energies.append(theta)
    return (state[None], jnp.stack(energies))


def solution(mesh):
    in_specs = (
        P("sector", None, None, None),
        P("term", "sector", None, None),
        P("term", "sector", None, None),
        P("sector", None, None, None),
        P(),
    )
    out_specs = (P("sector", None, None, None), P())
    return jax.shard_map(local, mesh=mesh, in_specs=in_specs, out_specs=out_specs, check_vma=False)
```

profile of v0, /device:TPU:0, one launch (start us, length us, event | category | flops | bytes accessed | tf_op | source)
XLA Modules:
  0.0 424.9 jit_solution(16946019127858269423)
XLA Ops:
  7.2 0.0 copy-start
  7.2 0.0 all-reduce.7.cloned.1.call-start
  7.2 0.0 copy-start.6
  7.2 0.6 copy-done.6
  7.9 0.1 iota_compare_fusion
  8.0 0.0 copy-start.5
  8.0 1.1 copy.7
  9.1 0.0 copy-done.5
  9.1 16.6 %all_gather.3 = bf16[2,8,128,128]{3,2,1,0:T(8,128)(2,1)S(1)} all-gather(bf16[2,1,128,128]{3,2,1,0:T(8,128)(2,1)S(1)} %copy-done.5), channel_id=1, replica_groups=mesh['term'=4,'sector'=8] {'sector'}, dimensions={1}, use_global_device_ids=true | all-gather | bytes 589824 | tf_op jit(solution)/shard_map/all_gather | solution.py:41
  25.7 0.0 copy-done
  25.7 1.2 fusion.8
  27.0 0.0 copy-start.4
  27.0 0.0 all-reduce.7.cloned.1.call-update
  27.0 0.0 all-reduce.9.cloned.1.call-start
  27.1 0.9 copy-done.4
  27.9 0.2 copy.8
  28.1 43.0 %all-reduce.7.cloned.1.call-done = bf16[8,128,128]{1,2,0:T(8,128)(2,1)} async-done(((bf16[8,128,128]{1,2,0:T(8,128)(2,1)}), bf16[8,128,128]{1,2,0:T(8,128)(2,1)}) %all-reduce.7.cloned.1.call-update) | async-done | bytes 262160 | tf_op jit(solution)/shard_map/psum | solution.py:51
  71.1 1.2 fusion.34
  72.3 0.6 multiply_reduce_fusion.4
  72.9 0.0 copy-start.1
  72.9 39.6 %all-reduce.2 = (f32[]{:T(128)}, f32[]{:T(128)}) all-reduce(f32[]{:T(128)} %get-tuple-element.9, f32[]{:T(128)} %get-tuple-element.8), channel_id=1, replica_groups=mesh['term'=4,'sector'=8] {'term','sector'}, use_global_device_ids=true, to_apply=%region_2.0 | all-reduce | flops 2 | bytes 16 | tf_op jit(solution)/shard_map/psum | solution.py:17
  113.9 0.7 fusion.43
  114.5 41.4 %psum.87 = f32[]{:T(128)} all-reduce(f32[]{:T(128)} %fusion.43), channel_id=1, replica_groups=mesh['term'=4,'sector'=8] {'term','sector'}, use_global_device_ids=true, to_apply=%region_6.0 | all-reduce | flops 1 | bytes 8 | tf_op jit(solution)/shard_map/psum | solution.py:22
  156.6 0.0 copy-done.1
  156.6 0.3 fusion.52
  156.9 1.2 fusion.7
  158.1 0.0 all-reduce.9.cloned.1.call-update
  158.1 0.0 all-reduce.11.cloned.1.call-start
  158.1 43.0 %all-reduce.9.cloned.1.call-done = bf16[8,128,128]{1,2,0:T(8,128)(2,1)} async-done(((bf16[8,128,128]{1,2,0:T(8,128)(2,1)}), bf16[8,128,128]{1,2,0:T(8,128)(2,1)}) %all-reduce.9.cloned.1.call-update) | async-done | bytes 262160 | tf_op jit(solution)/shard_map/psum | solution.py:51
  201.2 1.1 and_select_fusion.1
  202.3 0.6 multiply_reduce_fusion.2
  203.0 39.6 %all-reduce.1 = (f32[]{:T(128)}, f32[]{:T(128)}) all-reduce(f32[]{:T(128)} %get-tuple-element.7, f32[]{:T(128)} %get-tuple-element.6), channel_id=1, replica_groups=mesh['term'=4,'sector'=8] {'term','sector'}, use_global_device_ids=true, to_apply=%region_9.0 | all-reduce | flops 2 | bytes 16 | tf_op jit(solution)/shard_map/psum | solution.py:17
  243.9 0.7 fusion.42
  244.5 41.4 %psum.91 = f32[]{:T(128)} all-reduce(f32[]{:T(128)} %fusion.42), channel_id=1, replica_groups=mesh['term'=4,'sector'=8] {'term','sector'}, use_global_device_ids=true, to_apply=%region_13.0 | all-reduce | flops 1 | bytes 8 | tf_op jit(solution)/shard_map/psum | solution.py:22
  286.6 0.0 copy-done.3
  286.6 0.3 fusion.50
  286.9 1.2 fusion.6
  288.1 0.0 all-reduce.11.cloned.1.call-update
  288.1 43.1 %all-reduce.11.cloned.1.call-done = bf16[8,128,128]{1,2,0:T(8,128)(2,1)} async-done(((bf16[8,128,128]{1,2,0:T(8,128)(2,1)}), bf16[8,128,128]{1,2,0:T(8,128)(2,1)}) %all-reduce.11.cloned.1.call-update) | async-done | bytes 262160 | tf_op jit(solution)/shard_map/psum | solution.py:51
  331.2 1.1 and_select_fusion
  332.3 0.6 multiply_reduce_fusion
  333.0 39.6 %all-reduce = (f32[]{:T(128)}, f32[]{:T(128)}) all-reduce(f32[]{:T(128)} %get-tuple-element.5, f32[]{:T(128)} %get-tuple-element.4), channel_id=1, replica_groups=mesh['term'=4,'sector'=8] {'term','sector'}, use_global_device_ids=true, to_apply=%region_16.0 | all-reduce | flops 2 | bytes 16 | tf_op jit(solution)/shard_map/psum | solution.py:17
  373.9 0.7 fusion.41
  374.5 41.4 %psum.95 = f32[]{:T(128)} all-reduce(f32[]{:T(128)} %fusion.41), channel_id=1, replica_groups=mesh['term'=4,'sector'=8] {'term','sector'}, use_global_device_ids=true, to_apply=%region_20.0 | all-reduce | flops 1 | bytes 8 | tf_op jit(solution)/shard_map/psum | solution.py:22
  416.6 0.0 copy-done.2
  416.6 0.3 fusion.31
  416.9 0.9 copy.9
  417.7 0.6 pad_maximum_fusion
  (4 shorter events, 0.0 us)
Async XLA Ops:
  7.2 18.6 %copy-start = (bf16[2,1,128,128]{3,2,1,0:T(8,128)(2,1)S(1)}, bf16[2,1,128,128]{3,2,1,0:T(8,128)(2,1)}, u32[]{:S(2)}) copy-start(bf16[2,1,128,128]{3,2,1,0:T(8,128)(2,1)} %param.6) | copy-start | bytes 196612
  7.2 64.0 %all-reduce.7.cloned.1.call-start = ((), (), s32[]{:S(2)}) async-start(), calls=%async_computation | async-start | bytes 524288 | tf_op jit(solution)/shard_map/psum | solution.py:51
  7.2 0.7 copy-start.6
  8.0 1.2 copy-start.5
  27.0 0.9 copy-start.4
  27.0 174.2 %all-reduce.9.cloned.1.call-start = ((), (), s32[]{:S(2)}) async-start(), calls=%async_computation.1 | async-start | bytes 524288 | tf_op jit(solution)/shard_map/psum | solution.py:51
  72.9 83.6 %copy-start.1 = (bf16[8,128,128]{1,2,0:T(8,128)(2,1)S(1)}, bf16[8,128,128]{1,2,0:T(8,128)(2,1)}, u32[]{:S(2)}) copy-start(bf16[8,128,128]{1,2,0:T(8,128)(2,1)} %all-reduce.7.cloned.1.call-done) | copy-start | bytes 786436
  158.1 173.1 %all-reduce.11.cloned.1.call-start = ((), (), s32[]{:S(2)}) async-start(), calls=%async_computation.2 | async-start | bytes 524288 | tf_op jit(solution)/shard_map/psum | solution.py:51
  203.0 83.6 %copy-start.3 = (bf16[8,128,128]{1,2,0:T(8,128)(2,1)S(1)}, bf16[8,128,128]{1,2,0:T(8,128)(2,1)}, u32[]{:S(2)}) copy-start(bf16[8,128,128]{1,2,0:T(8,128)(2,1)} %all-reduce.9.cloned.1.call-done) | copy-start | bytes 786436
  333.0 83.6 %copy-start.2 = (bf16[8,128,128]{1,2,0:T(8,128)(2,1)S(1)}, bf16[8,128,128]{1,2,0:T(8,128)(2,1)}, u32[]{:S(2)}) copy-start(bf16[8,128,128]{1,2,0:T(8,128)(2,1)} %all-reduce.11.cloned.1.call-done) | copy-start | bytes 786436
Sparse Core Ops, SparseCore 0:
  27.1 43.9 all-reduce.6
  158.2 42.9 all-reduce.8
  288.2 42.9 all-reduce.10
where the time goes:
time: 426 us; the launch traced here: 425 us
  blocking collectives  259 us (61%)
  waiting for transfers between devices  129 us (30%)
  between operations  20 us (5%)
  other arithmetic  8.96 us (2%)
    psum x3, waiting for transfers between devices, local(): lax.psum(partial_value.astype(jnp.bfloat16), 'term').astype(jnp.float32)  129 us
    psum x3, blocking collectives, dot_sums(): squares = lax.psum(jnp.sum(fresh * fresh), ('term', 'sector'))  124 us
    psum x3, blocking collectives, dot_sums(): lax.psum((jnp.sum(cur_share * cur_share), jnp.sum(cur_share * img_share))...  119 us
    all_gather x1, blocking collectives, local(): right_all = lax.all_gather(right_env, 'sector', axis=1, tiled=True)  16.6 us
  transfers between devices with their start and end apart: 3, of which 3 were waited for; matrix products, arithmetic and copies ran while one was open for 0% of the time, Pallas kernels for 0%

commit v1 on v0

--- a/solution.py
+++ b/solution.py
@@ -4,6 +4,22 @@
 from jax.sharding import PartitionSpec as P
 
 ITERS = 3
+
+
+def series_handle(vector, device_axis):
+    dev_n = lax.axis_size(device_axis)
+    stack_in = [(s, (s + 1) % dev_n) for s in range(dev_n)]
+
+    def solve_record(piece_out):
+        if len(piece_out) == dev_n:
+            return piece_out
+        everything = lax.ppermute(piece_out[0], device_axis, stack_in)
+        return solve_record([everything, *piece_out])
+
+    now = solve_record([vector])
+    e_now = jnp.concatenate(now, axis=1)
+    latest = lax.axis_index(device_axis)
+    return jnp.roll(e_now, (latest + 1) * vector.shape[1], axis=1)
 
 
 def block_mask(block_sizes, width, own_row):
@@ -38,7 +54,7 @@
     def portion(values):
         return lax.dynamic_slice_in_dim(values, share_start, share, 0)
 
-    right_all = lax.all_gather(right_env, "sector", axis=1, tiled=True)
+    right_all = series_handle(right_env, "sector")
     energies = []
     for step in range(ITERS):
         images = jnp.einsum(

time: 426 us -> 446 us (1.047)
  waiting for transfers between devices: 129 us -> 164 us
  blocking collectives: 259 us -> 243 us
    ppermute x0 -> x7, waiting for transfers between devices: none -> 37.2 us  [solve_record(): everything = lax.ppermute(piece_out[0], device_axis, stack_in)]
    all_gather x1 -> x0, blocking collectives: 16.6 us -> none  [local(): right_all = lax.all_gather(right_env, 'sector', axis=1, tiled=True)]
  transfers between devices with their start and end apart: 3 -> 10, of which waited for: 3 -> 10; matrix products, arithmetic and copies ran while one was open for 0% -> 0% of each run, Pallas kernels for 0% -> 0%
where the time goes in v1:
time: 446 us; the launch traced here: 445 us
  blocking collectives  243 us (54%)
  waiting for transfers between devices  164 us (37%)
  between operations  20 us (4%)
  other arithmetic  9.61 us (2%)
    psum x3, waiting for transfers between devices, local(): lax.psum(partial_value.astype(jnp.bfloat16), 'term').astype(jnp.float32)  127 us
    psum x3, blocking collectives, dot_sums(): squares = lax.psum(jnp.sum(fresh * fresh), ('term', 'sector'))  124 us
    psum x3, blocking collectives, dot_sums(): lax.psum((jnp.sum(cur_share * cur_share), jnp.sum(cur_share * img_share))...  119 us
    ppermute x7, waiting for transfers between devices, solve_record(): everything = lax.ppermute(piece_out[0], device_axis, stack_in)  37.2 us
  transfers between devices with their start and end apart: 10, of which 10 were waited for; matrix products, arithmetic and copies ran while one was open for 0% of the time, Pallas kernels for 0%

profile of v1, /device:TPU:0, one launch (start us, length us, event | category | flops | bytes accessed | tf_op | source)
XLA Modules:
  0.0 444.9 jit_solution(5949829578810973409)
XLA Ops:
  7.2 0.0 copy-start
  7.2 0.0 all-reduce.7.cloned.1.call-start
  7.2 0.5 collective-permute-start
  7.7 6.2 %collective-permute-done = bf16[2,1,128,128]{3,2,1,0:T(8,128)(2,1)S(1)} collective-permute-done((bf16[2,1,128,128]{3,2,1,0:T(8,128)(2,1)}, bf16[2,1,128,128]{3,2,1,0:T(8,128)(2,1)S(1)}, u32[]{:S(2)}, u32[]{:S(2)}) %collective-permute-start) | collective-permute-done | bytes 65568 | tf_op jit(solution)/shard_map/ppermute | solution.py:16
  13.9 5.5 %collective-permute-done.1 = bf16[2,1,128,128]{3,2,1,0:T(8,128)(2,1)S(1)} collective-permute-done((bf16[2,1,128,128]{3,2,1,0:T(8,128)(2,1)S(1)}, bf16[2,1,128,128]{3,2,1,0:T(8,128)(2,1)S(1)}, u32[]{:S(2)}, u32[]{:S(2)}) %collective-permute-start.1) | collective-permute-done | bytes 65568 | tf_op jit(solution)/shard_map/ppermute | solution.py:16
  19.4 0.0 collective-permute-start.2
  19.4 5.5 %collective-permute-done.2 = bf16[2,1,128,128]{3,2,1,0:T(8,128)(2,1)S(1)} collective-permute-done((bf16[2,1,128,128]{3,2,1,0:T(8,128)(2,1)S(1)}, bf16[2,1,128,128]{3,2,1,0:T(8,128)(2,1)S(1)}, u32[]{:S(2)}, u32[]{:S(2)}) %collective-permute-start.2) | collective-permute-done | bytes 65568 | tf_op jit(solution)/shard_map/ppermute | solution.py:16
  24.9 5.5 %collective-permute-done.3 = bf16[2,1,128,128]{3,2,1,0:T(8,128)(2,1)S(1)} collective-permute-done((bf16[2,1,128,128]{3,2,1,0:T(8,128)(2,1)S(1)}, bf16[2,1,128,128]{3,2,1,0:T(8,128)(2,1)S(1)}, u32[]{:S(2)}, u32[]{:S(2)}) %collective-permute-start.3) | collective-permute-done | bytes 65568 | tf_op jit(solution)/shard_map/ppermute | solution.py:16
  30.4 5.5 %collective-permute-done.4 = bf16[2,1,128,128]{3,2,1,0:T(8,128)(2,1)S(1)} collective-permute-done((bf16[2,1,128,128]{3,2,1,0:T(8,128)(2,1)S(1)}, bf16[2,1,128,128]{3,2,1,0:T(8,128)(2,1)S(1)}, u32[]{:S(2)}, u32[]{:S(2)}) %collective-permute-start.4) | collective-permute-done | bytes 65568 | tf_op jit(solution)/shard_map/ppermute | solution.py:16
  35.9 0.7 iota_compare_fusion
  36.6 1.1 copy.7
  37.7 3.6 collective-permute-done.5
  41.4 5.5 %collective-permute-done.6 = bf16[2,1,128,128]{3,2,1,0:T(8,128)(2,1)S(1)} collective-permute-done((bf16[2,1,128,128]{3,2,1,0:T(8,128)(2,1)S(1)}, bf16[2,1,128,128]{3,2,1,0:T(8,128)(2,1)S(1)}, u32[]{:S(2)}, u32[]{:S(2)}) %collective-permute-start.6) | collective-permute-done | bytes 65568 | tf_op jit(solution)/shard_map/ppermute | solution.py:16
  47.0 0.0 copy-start.5
  47.0 0.8 copy-done.5
  48.0 1.3 fusion.8
  49.3 0.0 all-reduce.7.cloned.1.call-update
  49.3 0.0 all-reduce.9.cloned.1.call-start
  49.4 0.9 copy-done.4
  50.3 0.2 copy.8
  50.5 40.7 %all-reduce.7.cloned.1.call-done = bf16[8,128,128]{1,2,0:T(8,128)(2,1)} async-done(((bf16[8,128,128]{1,2,0:T(8,128)(2,1)}), bf16[8,128,128]{1,2,0:T(8,128)(2,1)}) %all-reduce.7.cloned.1.call-update) | async-done | bytes 262160 | tf_op jit(solution)/shard_map/psum | solution.py:67
  91.2 1.2 fusion.34
  92.3 0.6 multiply_reduce_fusion.4
  93.0 39.6 %all-reduce.2 = (f32[]{:T(128)}, f32[]{:T(128)}) all-reduce(f32[]{:T(128)} %get-tuple-element.9, f32[]{:T(128)} %get-tuple-element.8), channel_id=1, replica_groups=mesh['term'=4,'sector'=8] {'term','sector'}, use_global_device_ids=true, to_apply=%region_2.3 | all-reduce | flops 2 | bytes 16 | tf_op jit(solution)/shard_map/psum | solution.py:33
  133.9 0.7 fusion.43
  134.5 41.4 %psum.87 = f32[]{:T(128)} all-reduce(f32[]{:T(128)} %fusion.43), channel_id=1, replica_groups=mesh['term'=4,'sector'=8] {'term','sector'}, use_global_device_ids=true, to_apply=%region_6.7 | all-reduce | flops 1 | bytes 8 | tf_op jit(solution)/shard_map/psum | solution.py:38
  176.6 0.3 fusion.52
  176.9 1.2 fusion.7
  178.1 0.0 all-reduce.9.cloned.1.call-update
  178.1 0.0 all-reduce.11.cloned.1.call-start
  178.2 43.0 %all-reduce.9.cloned.1.call-done = bf16[8,128,128]{1,2,0:T(8,128)(2,1)} async-done(((bf16[8,128,128]{1,2,0:T(8,128)(2,1)}), bf16[8,128,128]{1,2,0:T(8,128)(2,1)}) %all-reduce.9.cloned.1.call-update) | async-done | bytes 262160 | tf_op jit(solution)/shard_map/psum | solution.py:67
  221.2 1.1 and_select_fusion.1
  222.3 0.6 multiply_reduce_fusion.2
  223.0 39.6 %all-reduce.1 = (f32[]{:T(128)}, f32[]{:T(128)}) all-reduce(f32[]{:T(128)} %get-tuple-element.7, f32[]{:T(128)} %get-tuple-element.6), channel_id=1, replica_groups=mesh['term'=4,'sector'=8] {'term','sector'}, use_global_device_ids=true, to_apply=%region_9.10 | all-reduce | flops 2 | bytes 16 | tf_op jit(solution)/shard_map/psum | solution.py:33
  263.9 0.7 fusion.42
  264.5 41.4 %psum.91 = f32[]{:T(128)} all-reduce(f32[]{:T(128)} %fusion.42), channel_id=1, replica_groups=mesh['term'=4,'sector'=8] {'term','sector'}, use_global_device_ids=true, to_apply=%region_13.14 | all-reduce | flops 1 | bytes 8 | tf_op jit(solution)/shard_map/psum | solution.py:38
  306.6 0.3 fusion.50
  306.9 1.2 fusion.6
  308.1 0.0 all-reduce.11.cloned.1.call-update
  308.1 43.1 %all-reduce.11.cloned.1.call-done = bf16[8,128,128]{1,2,0:T(8,128)(2,1)} async-done(((bf16[8,128,128]{1,2,0:T(8,128)(2,1)}), bf16[8,128,128]{1,2,0:T(8,128)(2,1)}) %all-reduce.11.cloned.1.call-update) | async-done | bytes 262160 | tf_op jit(solution)/shard_map/psum | solution.py:67
  351.2 1.1 and_select_fusion
  352.4 0.6 multiply_reduce_fusion
  353.0 39.6 %all-reduce = (f32[]{:T(128)}, f32[]{:T(128)}) all-reduce(f32[]{:T(128)} %get-tuple-element.5, f32[]{:T(128)} %get-tuple-element.4), channel_id=1, replica_groups=mesh['term'=4,'sector'=8] {'term','sector'}, use_global_device_ids=true, to_apply=%region_16.17 | all-reduce | flops 2 | bytes 16 | tf_op jit(solution)/shard_map/psum | solution.py:33
  393.9 0.7 fusion.41
  394.6 41.4 %psum.95 = f32[]{:T(128)} all-reduce(f32[]{:T(128)} %fusion.41), channel_id=1, replica_groups=mesh['term'=4,'sector'=8] {'term','sector'}, use_global_device_ids=true, to_apply=%region_20.21 | all-reduce | flops 1 | bytes 8 | tf_op jit(solution)/shard_map/psum | solution.py:38
  436.6 0.3 fusion.31
  436.9 0.9 copy.9
  437.8 0.6 pad_maximum_fusion
  (32 shorter events, 0.3 us)
Async XLA Ops:
  7.2 40.9 %copy-start = (bf16[2,1,128,128]{3,2,1,0:T(8,128)(2,1)S(1)}, bf16[2,1,128,128]{3,2,1,0:T(8,128)(2,1)}, u32[]{:S(2)}) copy-start(bf16[2,1,128,128]{3,2,1,0:T(8,128)(2,1)} %param.6) | copy-start | bytes 196612
  7.2 84.0 %all-reduce.7.cloned.1.call-start = ((), (), s32[]{:S(2)}) async-start(), calls=%async_computation | async-start | bytes 524288 | tf_op jit(solution)/shard_map/psum | solution.py:67
  7.2 6.7 %collective-permute-start = (bf16[2,1,128,128]{3,2,1,0:T(8,128)(2,1)}, bf16[2,1,128,128]{3,2,1,0:T(8,128)(2,1)S(1)}, u32[]{:S(2)}, u32[]{:S(2)}) collective-permute-start(bf16[2,1,128,128]{3,2,1,0:T(8,128)(2,1)} %param.7), channel_id=1, source_target_pairs={{0,1},{1,2},{2,3},{3,4},{4,5},{5,6},{6,7},{7,0},{8,9},{9,10},{10,1... | collective-permute-start | bytes 196616 | tf_op jit(solution)/shard_map/ppermute | solution.py:16
  13.9 5.5 %collective-permute-start.1 = (bf16[2,1,128,128]{3,2,1,0:T(8,128)(2,1)S(1)}, bf16[2,1,128,128]{3,2,1,0:T(8,128)(2,1)S(1)}, u32[]{:S(2)}, u32[]{:S(2)}) collective-permute-start(bf16[2,1,128,128]{3,2,1,0:T(8,128)(2,1)S(1)} %collective-permute-done), channel_id=1, source_target_pairs={{0,1},{1,2},{2,3},{3,4},{4,5},{5,6},{6,7},{7,0},{8,9},{9,10},{10,1... | collective-permute-start | bytes 196616 | tf_op jit(solution)/shard_map/ppermute | solution.py:16
  19.4 5.5 %collective-permute-start.2 = (bf16[2,1,128,128]{3,2,1,0:T(8,128)(2,1)S(1)}, bf16[2,1,128,128]{3,2,1,0:T(8,128)(2,1)S(1)}, u32[]{:S(2)}, u32[]{:S(2)}) collective-permute-start(bf16[2,1,128,128]{3,2,1,0:T(8,128)(2,1)S(1)} %collective-permute-done.1), channel_id=1, source_target_pairs={{0,1},{1,2},{2,3},{3,4},{4,5},{5,6},{6,7},{7,0},{8,9},{9,10},{10,1... | collective-permute-start | bytes 196616 | tf_op jit(solution)/shard_map/ppermute | solution.py:16
  24.9 5.5 %collective-permute-start.3 = (bf16[2,1,128,128]{3,2,1,0:T(8,128)(2,1)S(1)}, bf16[2,1,128,128]{3,2,1,0:T(8,128)(2,1)S(1)}, u32[]{:S(2)}, u32[]{:S(2)}) collective-permute-start(bf16[2,1,128,128]{3,2,1,0:T(8,128)(2,1)S(1)} %collective-permute-done.2), channel_id=1, source_target_pairs={{0,1},{1,2},{2,3},{3,4},{4,5},{5,6},{6,7},{7,0},{8,9},{9,10},{10,1... | collective-permute-start | bytes 196616 | tf_op jit(solution)/shard_map/ppermute | solution.py:16
  30.4 5.5 %collective-permute-start.4 = (bf16[2,1,128,128]{3,2,1,0:T(8,128)(2,1)S(1)}, bf16[2,1,128,128]{3,2,1,0:T(8,128)(2,1)S(1)}, u32[]{:S(2)}, u32[]{:S(2)}) collective-permute-start(bf16[2,1,128,128]{3,2,1,0:T(8,128)(2,1)S(1)} %collective-permute-done.3), channel_id=1, source_target_pairs={{0,1},{1,2},{2,3},{3,4},{4,5},{5,6},{6,7},{7,0},{8,9},{9,10},{10,1... | collective-permute-start | bytes 196616 | tf_op jit(solution)/shard_map/ppermute | solution.py:16
  35.9 5.5 %collective-permute-start.5 = (bf16[2,1,128,128]{3,2,1,0:T(8,128)(2,1)S(1)}, bf16[2,1,128,128]{3,2,1,0:T(8,128)(2,1)S(1)}, u32[]{:S(2)}, u32[]{:S(2)}) collective-permute-start(bf16[2,1,128,128]{3,2,1,0:T(8,128)(2,1)S(1)} %collective-permute-done.4), channel_id=1, source_target_pairs={{0,1},{1,2},{2,3},{3,4},{4,5},{5,6},{6,7},{7,0},{8,9},{9,10},{10,1... | collective-permute-start | bytes 196616 | tf_op jit(solution)/shard_map/ppermute | solution.py:16
  41.4 5.5 %collective-permute-start.6 = (bf16[2,1,128,128]{3,2,1,0:T(8,128)(2,1)S(1)}, bf16[2,1,128,128]{3,2,1,0:T(8,128)(2,1)S(1)}, u32[]{:S(2)}, u32[]{:S(2)}) collective-permute-start(bf16[2,1,128,128]{3,2,1,0:T(8,128)(2,1)S(1)} %collective-permute-done.5), channel_id=1, source_target_pairs={{0,1},{1,2},{2,3},{3,4},{4,5},{5,6},{6,7},{7,0},{8,9},{9,10},{10,1... | collective-permute-start | bytes 196616 | tf_op jit(solution)/shard_map/ppermute | solution.py:16
  47.0 0.8 copy-start.5
  49.3 0.9 copy-start.4
  49.3 171.8 %all-reduce.9.cloned.1.call-start = ((), (), s32[]{:S(2)}) async-start(), calls=%async_computation.1 | async-start | bytes 524288 | tf_op jit(solution)/shard_map/psum | solution.py:67
  93.0 83.6 %copy-start.1 = (bf16[8,128,128]{1,2,0:T(8,128)(2,1)S(1)}, bf16[8,128,128]{1,2,0:T(8,128)(2,1)}, u32[]{:S(2)}) copy-start(bf16[8,128,128]{1,2,0:T(8,128)(2,1)} %all-reduce.7.cloned.1.call-done) | copy-start | bytes 786436
  178.1 173.1 %all-reduce.11.cloned.1.call-start = ((), (), s32[]{:S(2)}) async-start(), calls=%async_computation.2 | async-start | bytes 524288 | tf_op jit(solution)/shard_map/psum | solution.py:67
  223.0 83.6 %copy-start.3 = (bf16[8,128,128]{1,2,0:T(8,128)(2,1)S(1)}, bf16[8,128,128]{1,2,0:T(8,128)(2,1)}, u32[]{:S(2)}) copy-start(bf16[8,128,128]{1,2,0:T(8,128)(2,1)} %all-reduce.9.cloned.1.call-done) | copy-start | bytes 786436
  353.0 83.6 %copy-start.2 = (bf16[8,128,128]{1,2,0:T(8,128)(2,1)S(1)}, bf16[8,128,128]{1,2,0:T(8,128)(2,1)}, u32[]{:S(2)}) copy-start(bf16[8,128,128]{1,2,0:T(8,128)(2,1)} %all-reduce.11.cloned.1.call-done) | copy-start | bytes 786436
Sparse Core Ops, SparseCore 0:
  49.5 41.6 all-reduce.6
  178.2 42.8 all-reduce.8
  308.3 42.9 all-reduce.10
